TPU v7x, 32 devices: a whole 2x2x4 slice. The times are simulated.
32 devices in a mesh: clu: 8 (over z, y), grp: 4 (over x, core).
Axes of the slice: x: 2, y: 2, z: 4, core: 2. Of those that a mesh axis runs over, the one named last changes fastest.
Arguments:
- embeddings: bfloat16 [16384, 768], P(('clu', 'grp')), may hold values from -6 to 6
- cluster_of: int32 [16384], P(('clu', 'grp')), may hold values from 0 to 15, as said below
- new_rows: bfloat16 [512, 768], P(('clu', 'grp')), may hold values from -6 to 6
- centroids: bfloat16 [8192, 768], P(('clu', 'grp')), may hold values from -6 to 6
Outputs:
- dup_score: float32 [16384], P(('clu', 'grp'))
- centroid_score: float32 [512], P(('clu', 'grp'))
Inputs may be any that keep to these rules, and one draw needn't show every extreme that they name: `cluster_of`: cluster k is owned by owner k mod 8; among the 512 rows of one device, at most 128 rows belong to the clusters of one owner, and in every such block some owner has exactly 128.
All inputs are finite; a program needn't handle non-finite values.
Results may differ from a plain program's by a relative error of at most 0.0015.
Values may be sent and summed in bfloat16 or wider, within the bound.
A program may use at most 64 MiB of HBM per device.

v0:
```python
import functools

import jax
import jax.numpy as jnp
from jax import lax
from jax.experimental import pallas as pl
from jax.experimental.pallas import tpu as pltpu
from jax.sharding import PartitionSpec as P

epsilon = 1e-06
lanes = 128
chunk_order = (0, 1, 2, 3, 4, 5, 6, 7)
chunk_count = len(chunk_order)
stage_count = chunk_count // 2
MESH = pl.DeviceIdType.MESH


def normalize(values):
    wide = values.astype(jnp.float32)
    total = jnp.sum(wide * wide, axis=-1, keepdims=True)
    return (wide * lax.rsqrt(total + epsilon)).astype(jnp.bfloat16)


def pair_scores(left_units, right_units):
    return lax.dot_general(
        left_units, right_units, (((1,), (1,)), ((), ())), preferred_element_type=jnp.float32
    )


def exchange_kernel(
    clu_count,
    cap,
    new_count,
    emb_hbm,
    cluster_hbm,
    new_hbm,
    cent_hbm,
    dup_ref,
    best_ref,
    emb_ref,
    cluster_ref,
    new_ref,
    cent_ref,
    units,
    send_ref,
    ids_ref,
    held,
    held_ids,
    marks,
    id_rows,
    own_acc,
    mate_acc,
    mate_in,
    new_held,
    cent_unit,
    part,
    part_in,
    message,
    message_in,
    local_sem,
    data_send,
    data_recv,
    id_send,
    id_recv,
    new_send,
    new_recv,
    fwd_send,
    fwd_recv,
    fwd_id_send,
    fwd_id_recv,
    wide_send,
    wide_recv,
    part_send,
    part_recv,
    mate_send,
    mate_recv,
    msg_send,
    msg_recv,
):
    per_chunk = clu_count // chunk_count
    half = lanes
    stage_rows = 2 * half
    me = lax.axis_index("clu")
    grp = lax.axis_index("grp")

    def far(block):
        chunk, inner = divmod(block, per_chunk)
        return {"clu": me ^ (chunk_order[chunk] * per_chunk + inner), "grp": grp}

    def near(step):
        return {"clu": me, "grp": grp ^ step}

    def chunk_row(chunk, kind):
        stage, part_of = divmod(chunk, 2)
        return stage * 3 * stage_rows + kind * stage_rows + part_of * half

    def block_rows(block):
        chunk, inner = divmod(block, per_chunk)
        return pl.ds(chunk_row(chunk, 0) + inner * cap, cap)

    def remote(src, dst, send_sem, recv_sem, device):
        return pltpu.make_async_remote_copy(
            src_ref=src,
            dst_ref=dst,
            send_sem=send_sem,
            recv_sem=recv_sem,
            device_id=device,
            device_id_type=MESH,
        )

    barrier = pltpu.get_barrier_semaphore()
    for block in range(1, clu_count):
        pl.semaphore_signal(barrier, inc=1, device_id=far(block), device_id_type=MESH)
    for step in (1, 2, 3):
        pl.semaphore_signal(barrier, inc=1, device_id=near(step), device_id_type=MESH)

    local = [
        pltpu.make_async_copy(new_hbm, new_ref, local_sem.at[0]),
        pltpu.make_async_copy(cluster_hbm, cluster_ref, local_sem.at[1]),
        pltpu.make_async_copy(emb_hbm, emb_ref, local_sem.at[2]),
        pltpu.make_async_copy(cent_hbm, cent_ref, local_sem.at[3]),
    ]
    for copy in local:
        copy.start()

    new_copies = []
    data_copies = [None]
    id_copies = [None]
    for block in range(1, clu_count):
        new_copies.append(
            remote(
                new_held.at[0, pl.ds(0, new_count)],
                new_held.at[0, pl.ds(block * new_count, new_count)],
                new_send.at[block],
                new_recv.at[block],
                far(block),
            )
        )
        id_copies.append(
            remote(
                ids_ref.at[block],
                held_ids.at[0, block],
                id_send.at[block],
                id_recv.at[block],
                far(block),
            )
        )
        data_copies.append(
            remote(
                send_ref.at[pl.ds(block * cap, cap)],
                held.at[block_rows(block)],
                data_send.at[block],
                data_recv.at[block],
                far(block),
            )
        )

    local[0].wait()
    new_held[0, 0:new_count, :] = normalize(new_ref[...])
    local[1].wait()
    cluster = cluster_ref[...]
    rows = cluster.shape[1]
    distance = (cluster & (clu_count - 1)) ^ me
    far_chunk = distance // per_chunk
    place = jnp.zeros_like(distance)
    for index, chunk in enumerate(chunk_order):
        place = jnp.where(far_chunk == chunk, index, place)
    place = place * per_chunk + distance % per_chunk
    owner_hot = lax.broadcasted_iota(jnp.int32, (clu_count, rows), 0) == place
    before = lax.broadcasted_iota(jnp.int32, (rows, rows), 0) < lax.broadcasted_iota(
        jnp.int32, (rows, rows), 1
    )
    preceding = jnp.dot(
        owner_hot.astype(jnp.bfloat16),
        before.astype(jnp.bfloat16),
        preferred_element_type=jnp.float32,
    )
    rank = jnp.sum(jnp.where(owner_hot, preceding, 0.0), axis=0, keepdims=True).astype(jnp.int32)
    slot = place * cap + rank
    id_values = jnp.broadcast_to((cluster + 1).astype(jnp.float32), (8, rows)).astype(jnp.bfloat16)
    chunk_slot = lax.broadcasted_iota(jnp.int32, (lanes, rows), 0)
    inner_block = lax.broadcasted_iota(jnp.int32, (8, lanes), 1) // cap
    local[2].wait()
    units[...] = normalize(emb_ref[...])
    pl.semaphore_wait(barrier, clu_count - 1 + 3)
    for copy in new_copies:
        copy.start()

    def pack(chunk):
        chosen = (chunk_slot + chunk * lanes == slot).astype(jnp.bfloat16)
        packed = jnp.dot(chosen, units[...], preferred_element_type=jnp.float32).astype(
            jnp.bfloat16
        )
        tile = pair_scores(id_values, chosen)
        for inner in range(per_chunk):
            block = chunk * per_chunk + inner
            if per_chunk == 1:
                own_tile = tile
            else:
                own_tile = jnp.where(inner_block == inner, tile, 0.0)
            if block == 0:
                held_ids[0, 0] = own_tile
                held[block_rows(0), :] = packed[0:cap]
            else:
                ids_ref[block] = own_tile
        if per_chunk > 1 or chunk > 0:
            send_ref[chunk * lanes : (chunk + 1) * lanes, :] = packed

    def dispatch(chunk):
        for block in range(max(1, chunk * per_chunk), (chunk + 1) * per_chunk):
            id_copies[block].start()
            data_copies[block].start()

    forwards = {}

    def spread_marks(chunk, kind):
        tile = held_ids[kind, chunk * per_chunk]
        for inner in range(1, per_chunk):
            tile = tile + held_ids[kind, chunk * per_chunk + inner]
        square = jnp.concatenate([tile] * (lanes // 8), axis=0)
        marks[pl.ds(chunk_row(chunk, kind), half), :] = jnp.transpose(square)
        if kind < 2:
            stage, part_of = divmod(chunk, 2)
            id_rows[stage, kind, :, pl.ds(part_of * half, half)] = tile

    def pass_on(chunk):
        for inner in range(per_chunk):
            block = chunk * per_chunk + inner
            if block > 0:
                id_copies[block].wait_recv()
                data_copies[block].wait_recv()
        src_rows = pl.ds(chunk_row(chunk, 0), half)
        src_ids = pl.ds(chunk * per_chunk, per_chunk)
        for kind in (2, 1):
            index = (kind - 1) * chunk_count + chunk
            ids = remote(
                held_ids.at[0, src_ids],
                held_ids.at[kind, src_ids],
                fwd_id_send.at[index],
                fwd_id_recv.at[index],
                near(kind),
            )
            data = remote(
                held.at[src_rows],
                held.at[pl.ds(chunk_row(chunk, kind), half)],
                fwd_send.at[index],
                fwd_recv.at[index],
                near(kind),
            )
            ids.start()
            data.start()
            forwards[chunk, kind] = (ids, data)
        spread_marks(chunk, 0)

    def receive(chunk):
        for kind in (1, 2):
            ids, data = forwards[chunk, kind]
            ids.wait_recv()
            data.wait_recv()
            spread_marks(chunk, kind)

    def fold(scores, matched):
        kept = jnp.where(matched, scores, -1.0)
        return jnp.max(kept.reshape(stage_rows // 8, 8, stage_rows), axis=0)

    def tile_rows(stage, kind):
        start = stage * (3 * stage_rows) + kind * stage_rows
        if not isinstance(start, int):
            start = pl.multiple_of(start, stage_rows)
        return pl.ds(start, stage_rows)

    def own_pair(kind, left, right):
        rows = tile_rows(left, kind)
        mark = marks[rows, :]
        matched = jnp.concatenate([mark, mark], axis=1) == id_rows[right, 0][0:1]
        if kind == 0:
            row_id = lax.broadcasted_iota(jnp.int32, (stage_rows, stage_rows), 0)
            col_id = lax.broadcasted_iota(jnp.int32, (stage_rows, stage_rows), 1)
            matched = matched & (row_id - col_id != (right - left) * stage_rows)
        scores = pair_scores(held[rows, :], held[tile_rows(right, 0), :])
        own_acc[right] = jnp.maximum(own_acc[right], fold(scores, matched))

    def mate_pair(left, right):
        rows = tile_rows(left, 2)
        mark = marks[rows, :]
        matched = jnp.concatenate([mark, mark], axis=1) == id_rows[right, 1][0:1]
        scores = pair_scores(held[rows, :], held[tile_rows(right, 1), :])
        mate_acc[right] = jnp.maximum(mate_acc[right], fold(scores, matched))

    def compute(stage):
        receive(2 * stage)
        receive(2 * stage + 1)

        def body(step, carry):
            left = jnp.minimum(step, stage)
            right = jnp.where(step <= stage, stage, step - stage - 1)
            for kind in range(3):
                own_pair(kind, left, right)
            mate_pair(left, right)
            return carry

        lax.fori_loop(0, 2 * stage + 1, body, 0)

    def compute_last():
        last = stage_count - 1

        def own_rows(step, carry):
            own_pair(0, last, step)
            return carry

        def own_cols(step, carry):
            for kind in range(3):
                own_pair(kind, step, last)
            return carry

        def other_rows(step, carry):
            own_pair(1, last, step)
            own_pair(2, last, step)
            mate_pair(last, step)
            return carry

        def mate_cols(step, carry):
            mate_pair(step, last)
            return carry

        lax.fori_loop(0, stage_count, own_rows, 0)
        lax.fori_loop(0, last, own_cols, 0)
        receive(2 * last)
        receive(2 * last + 1)
        lax.fori_loop(0, last, mate_cols, 0)
        lax.fori_loop(0, stage_count, other_rows, 0)

    group_rows = clu_count * new_count
    cross_new = remote(
        new_held.at[0], new_held.at[2], wide_send.at[0], wide_recv.at[0], near(2)
    )
    mate_new = remote(new_held.at[0], new_held.at[1], wide_send.at[1], wide_recv.at[1], near(1))
    corner_new = remote(new_held.at[2], new_held.at[3], wide_send.at[2], wide_recv.at[2], near(1))
    part_copies = [
        remote(
            part.at[step],
            part_in.at[step - 1],
            part_send.at[step - 1],
            part_recv.at[step - 1],
            near(step),
        )
        for step in (1, 2, 3)
    ]

    def new_first():
        for copy in new_copies:
            copy.wait_recv()
        cross_new.start()
        mate_new.start()

    def new_second():
        cross_new.wait_recv()
        corner_new.start()

    def new_third():
        mate_new.wait_recv()
        corner_new.wait_recv()
        for step in range(4):
            scores = pair_scores(cent_unit[...], new_held[step])
            top = jnp.max(
                scores.reshape(scores.shape[0] // 8, 8, group_rows), axis=0
            )
            top = jnp.max(top, axis=0, keepdims=True)
            if group_rows == lanes:
                part[step] = jnp.broadcast_to(top, (8, lanes))
            else:
                for row in range(group_rows // lanes):
                    part[step, row : row + 1, :] = top[:, row * lanes : (row + 1) * lanes]
        for copy in part_copies:
            copy.start()

    pack(0)
    for chunk in range(1, chunk_count):
        pack(chunk)
        if chunk == 1:
            if per_chunk > 1:
                dispatch(0)
        else:
            dispatch(chunk - 1)
    own_acc[...] = jnp.full(own_acc.shape, -1.0, jnp.float32)
    mate_acc[...] = jnp.full(mate_acc.shape, -1.0, jnp.float32)
    dispatch(chunk_count - 1)
    pass_on(0)
    local[3].wait()
    cent_unit[...] = normalize(cent_ref[...])
    pass_on(1)
    new_first()
    pass_on(2)
    pass_on(3)
    new_second()
    compute(0)
    pass_on(4)
    new_third()
    pass_on(5)
    compute(1)
    pass_on(6)
    compute(2)
    pass_on(7)
    compute_last()

    mate_copy = remote(mate_acc, mate_in, mate_send.at[0], mate_recv.at[0], near(1))
    mate_copy.start()
    cent_best = part[0]
    for step in (1, 2, 3):
        part_copies[step - 1].wait_recv()
        cent_best = jnp.maximum(cent_best, part_in[step - 1])
    mate_copy.wait_recv()
    for stage in range(stage_count):
        final = jnp.max(
            jnp.maximum(own_acc[stage], mate_in[stage]), axis=0, keepdims=True
        )
        for part_of in range(2):
            message[2 * stage + part_of, 0:8, :] = jnp.broadcast_to(
                final[:, part_of * half : (part_of + 1) * half], (8, lanes)
            )
            message[2 * stage + part_of, 8:, :] = cent_best
    messages = []
    for block in range(1, clu_count):
        copy = remote(
            message.at[block // per_chunk],
            message_in.at[block],
            msg_send.at[block],
            msg_recv.at[block],
            far(block),
        )
        copy.start()
        messages.append(copy)
    message_in[0] = message[0]
    for block in range(1, clu_count):
        new_copies[block - 1].wait_send()
        id_copies[block].wait_send()
        data_copies[block].wait_send()
    for ids, data in forwards.values():
        ids.wait_send()
        data.wait_send()
    for copy in (cross_new, mate_new, corner_new, mate_copy, *part_copies):
        copy.wait_send()
    for copy in messages:
        copy.wait()

    lane_block = lax.broadcasted_iota(jnp.int32, (1, lanes), 1) // cap
    row_list = []
    for chunk in range(chunk_count):
        row = message_in[chunk * per_chunk, 0:1, :]
        for inner in range(1, per_chunk):
            row = jnp.where(lane_block == inner, message_in[chunk * per_chunk + inner, 0:1, :], row)
        row_list.append(row)
    columns = jnp.transpose(
        jnp.concatenate([jnp.broadcast_to(row, (16, lanes)) for row in row_list], axis=0)
    )
    total = jnp.zeros(slot.shape, jnp.float32)
    position = lax.broadcasted_iota(jnp.int32, (lanes, slot.shape[1]), 0)
    for chunk in range(chunk_count):
        column = columns[:, chunk * 16 : chunk * 16 + 1]
        total = total + jnp.sum(
            jnp.where(position + chunk * lanes == slot, column, 0.0), axis=0, keepdims=True
        )
    dup_ref[...] = total
    best = None
    for block in range(clu_count):
        start = block * new_count
        row = 8 + start // lanes
        piece = message_in[block, row : row + 1, :][:, start % lanes : start % lanes + new_count]
        best = piece if best is None else jnp.maximum(best, piece)
    best_ref[...] = best


def shards(embeddings, cluster_of, new_rows, centroids):
    clu_count = lax.axis_size("clu")
    rows, width = embeddings.shape
    new_count = new_rows.shape[0]
    cap = 2 * rows // clu_count
    slots = clu_count * cap
    assert slots == chunk_count * lanes
    assert lax.axis_size("grp") == 4
    vmem = pl.BlockSpec(memory_space=pltpu.VMEM)
    anywhere = pl.BlockSpec(memory_space=pl.ANY)
    dma = pltpu.SemaphoreType.DMA
    group_rows = clu_count * new_count
    stage_rows = 2 * lanes
    dup, best = pl.pallas_call(
        functools.partial(exchange_kernel, clu_count, cap, new_count),
        out_shape=(
            jax.ShapeDtypeStruct((1, rows), jnp.float32),
            jax.ShapeDtypeStruct((1, new_count), jnp.float32),
        ),
        in_specs=[anywhere] * 4,
        out_specs=(vmem, vmem),
        scratch_shapes=[
            pltpu.VMEM((rows, width), jnp.bfloat16),
            pltpu.VMEM((1, rows), jnp.int32),
            pltpu.VMEM((new_count, width), jnp.bfloat16),
            pltpu.VMEM(centroids.shape, jnp.bfloat16),
            pltpu.VMEM((rows, width), jnp.bfloat16),
            pltpu.VMEM((slots, width), jnp.bfloat16),
            pltpu.VMEM((clu_count, 8, lanes), jnp.float32),
            pltpu.VMEM((3 * slots, width), jnp.bfloat16),
            pltpu.VMEM((3, clu_count, 8, lanes), jnp.float32),
            pltpu.VMEM((3 * slots, lanes), jnp.float32),
            pltpu.VMEM((stage_count, 2, 8, stage_rows), jnp.float32),
            pltpu.VMEM((stage_count, 8, stage_rows), jnp.float32),
            pltpu.VMEM((stage_count, 8, stage_rows), jnp.float32),
            pltpu.VMEM((stage_count, 8, stage_rows), jnp.float32),
            pltpu.VMEM((4, group_rows, width), jnp.bfloat16),
            pltpu.VMEM(centroids.shape, jnp.bfloat16),
            pltpu.VMEM((4, 8, lanes), jnp.float32),
            pltpu.VMEM((3, 8, lanes), jnp.float32),
            pltpu.VMEM((chunk_count, 16, lanes), jnp.float32),
            pltpu.VMEM((clu_count, 16, lanes), jnp.float32),
            dma((4,)),
            dma((clu_count,)),
            dma((clu_count,)),
            dma((clu_count,)),
            dma((clu_count,)),
            dma((clu_count,)),
            dma((clu_count,)),
            dma((2 * chunk_count,)),
            dma((2 * chunk_count,)),
            dma((2 * chunk_count,)),
            dma((2 * chunk_count,)),
            dma((3,)),
            dma((3,)),
            dma((3,)),
            dma((3,)),
            dma((1,)),
            dma((1,)),
            dma((clu_count,)),
            dma((clu_count,)),
        ],
        compiler_params=pltpu.CompilerParams(
            collective_id=0, has_side_effects=True, vmem_limit_bytes=67043328
        ),
        name="exchange",
    )(embeddings, cluster_of.reshape(1, rows), new_rows, centroids)
    return (dup.reshape(rows), best.reshape(new_count))


def solution(mesh):
    return jax.shard_map(
        shards,
        mesh=mesh,
        in_specs=(
            P(("clu", "grp"), None),
            P(("clu", "grp")),
            P(("clu", "grp"), None),
            P(("clu", "grp"), None),
        ),
        out_specs=(P(("clu", "grp")), P(("clu", "grp"))),
        check_vma=False,
    )
```

profile of v0, /device:TPU:0, one launch (start us, length us, event | category | flops | bytes accessed | tf_op | source)
XLA Modules:
  0.0 64.3 jit_solution(1197663055775004156)
XLA Ops:
  0.6 61.9 %exchange.1 = (f32[1,512]{1,0:T(1,128)}, f32[1,16]{1,0:T(1,128)}) custom-call(bf16[512,768]{1,0:T(8,128)(2,1)} %emb_hbm.1, s32[1,512]{1,0:T(1,128)} %bitcast.3, bf16[16,768]{1,0:T(8,128)(2,1)} %new_hbm.1, bf16[256,768]{1,0:T(8,128)(2,1)} %cent_hbm.1), custom_call_target="tpu_custom_call" | custom-call | tf_op jit(solution)/shard_map/exchange/pallas_call | solution.py:486
  62.5 0.0 copy-start
  62.5 0.7 %copy-done = f32[1,512]{1,0:T(1,128)S(1)} copy-done((f32[1,512]{1,0:T(1,128)S(1)}, f32[1,512]{1,0:T(1,128)}, u32[]{:S(2)}) %copy-start) | copy-done | bytes 2072
  63.2 0.0 copy-start.1
  63.2 0.6 copy.8
  63.8 0.1 copy-done.1
  63.8 0.5 copy.9
Async XLA Ops:
  62.5 0.7 %copy-start = (f32[1,512]{1,0:T(1,128)S(1)}, f32[1,512]{1,0:T(1,128)}, u32[]{:S(2)}) copy-start(f32[1,512]{1,0:T(1,128)} %get-tuple-element.4) | copy-start | bytes 6148
  63.2 0.6 copy-start.1
where the time goes:
time: 64.5 us; the launch traced here: 64.3 us
  Pallas kernels  61.9 us (96%)
  local copies, waits for them, and re-layouts  1.8 us (3%)
  between operations  0.65 us (1%)
    pallas_call x1, Pallas kernels, shards(): pl.pallas_call(functools.partial(exchange_kernel, clu_count, cap, new_cou...  61.9 us
    unnamed x6, local copies, waits for them, and re-layouts  1.8 us

commit v1 on v0

v1 whole, which is shorter than its diff:
```python
import functools

import jax
import jax.numpy as jnp
from jax import lax
from jax.experimental import pallas as pl
from jax.experimental.pallas import tpu as pltpu
from jax.sharding import PartitionSpec as P

epsilon = 1e-06
lanes = 128
send_chunks = 8
held_chunks = 2 * send_chunks
stage_count = held_chunks // 2
stage_rows = 2 * lanes
held_rows = held_chunks * lanes
spots_own = (0, 1, 2, 12)
spots_near = (3, 5, 7, 9)
spots_middle = (4, 6, 8, 10)
spots_outer = (11, 13, 14, 15)
MESH = pl.DeviceIdType.MESH


def normalize(values):
    wide = values.astype(jnp.float32)
    total = jnp.sum(wide * wide, axis=-1, keepdims=True)
    return (wide * lax.rsqrt(total + epsilon)).astype(jnp.bfloat16)


def pair_scores(left_units, right_units):
    return lax.dot_general(
        left_units, right_units, (((1,), (1,)), ((), ())), preferred_element_type=jnp.float32
    )


def exchange_kernel(
    clu_count,
    cap,
    new_count,
    emb_hbm,
    cluster_hbm,
    new_hbm,
    cent_hbm,
    dup_ref,
    best_ref,
    emb_ref,
    cluster_ref,
    new_ref,
    cent_ref,
    units,
    send_ref,
    relay_ref,
    ids_ref,
    held,
    held_ids,
    marks,
    id_rows,
    acc,
    new_all,
    cent_unit,
    part,
    part_in,
    best_out,
    best_in,
    message,
    message_in,
    local_sem,
    data_send,
    data_recv,
    hop_send,
    hop_recv,
    id_send,
    id_recv,
    fwd_send,
    fwd_recv,
    fwd_id_send,
    fwd_id_recv,
    new_send,
    new_recv,
    part_send,
    part_recv,
    best_send,
    best_recv,
    msg_send,
    msg_recv,
    cent_send,
    cent_recv,
):
    per_chunk = lanes // cap
    pieces = 2 if cap >= 32 else 1
    piece = cap // pieces
    cent_count = cent_hbm.shape[0]
    quarter = clu_count // 4
    codes = 2 * quarter
    group_chunks = send_chunks // 2
    group_rows = clu_count * new_count
    best_rows = group_rows // lanes
    me = lax.axis_index("clu")
    grp = lax.axis_index("grp")
    layer = me // quarter
    rest = me % quarter
    half = grp // 2
    inner = (layer == 1) | (layer == 2)
    outer = jnp.logical_not(inner)
    inner_bit = inner.astype(jnp.int32)
    self_place = codes

    def remote(src, dst, send_sem, recv_sem, device):
        return pltpu.make_async_remote_copy(
            src_ref=src,
            dst_ref=dst,
            send_sem=send_sem,
            recv_sem=recv_sem,
            device_id=device,
            device_id_type=MESH,
        )

    def far(step):
        return {"clu": me ^ step, "grp": grp}

    def near(step):
        return {"clu": me, "grp": grp ^ step}

    def related(to_layer, code):
        return {
            "clu": to_layer * quarter + (rest ^ (code // 2)),
            "grp": grp ^ (2 * (code % 2)),
        }

    first_layer = jnp.where(inner, layer ^ 3, layer ^ 1)
    second_layer = jnp.where(inner, layer, layer ^ 2)

    def owner_device(place):
        part_of, code = divmod(place, codes)
        return related(second_layer if part_of else first_layer, code)

    def owner_block(place):
        chunk, within = divmod(place, per_chunk)
        part_of, step = divmod(chunk, group_chunks)
        if part_of:
            spot = jnp.where(inner, spots_own[step], spots_outer[step])
        else:
            spot = jnp.where(inner, spots_middle[step], spots_near[step])
        return spot * per_chunk + within

    def held_source(spot):
        for to_layer, spots, part_of in (
            (layer, spots_own, 1),
            (layer ^ 1, spots_near, 0),
            (layer ^ 3, spots_middle, 0),
            (layer ^ 2, spots_outer, 1),
        ):
            if spot in spots:
                return to_layer, part_of * group_chunks + spots.index(spot)

    barrier = pltpu.get_barrier_semaphore()

    def greet(device):
        pl.semaphore_signal(barrier, inc=1, device_id=device, device_id_type=MESH)

    for step in range(1, clu_count):
        greet(far(step))
    for step in (1, 2, 3):
        greet(near(step))
    greeted = clu_count - 1 + 3
    for quarter_step in (0, 1, 2):
        for step in range(quarter):
            if quarter_step or step:
                greet({"clu": me ^ (quarter_step * quarter + step), "grp": grp ^ 2})
                greeted += 1

    @pl.when(inner)
    def _():
        for step in range(quarter):
            greet({"clu": me ^ (3 * quarter + step), "grp": grp ^ 2})

    local = [
        pltpu.make_async_copy(cluster_hbm, cluster_ref, local_sem.at[0]),
        pltpu.make_async_copy(emb_hbm, emb_ref, local_sem.at[1]),
        pltpu.make_async_copy(new_hbm, new_ref, local_sem.at[2]),
    ]
    for copy in local:
        copy.start()
    local_cent = pltpu.make_async_copy(
        cent_hbm, cent_ref.at[pl.ds(0, cent_count)], local_sem.at[3]
    )
    pl.when(outer)(local_cent.start)

    local[0].wait()
    cluster = cluster_ref[...]
    rows = cluster.shape[1]
    owner = cluster & (clu_count - 1)
    owner_layer = 1 + owner // codes
    second = (owner_layer == second_layer).astype(jnp.int32)
    place = second * codes + ((owner % codes) ^ (2 * rest + half))
    owner_hot = lax.broadcasted_iota(jnp.int32, (clu_count, rows), 0) == place
    before = lax.broadcasted_iota(jnp.int32, (rows, rows), 0) < lax.broadcasted_iota(
        jnp.int32, (rows, rows), 1
    )
    preceding = jnp.dot(
        owner_hot.astype(jnp.bfloat16),
        before.astype(jnp.bfloat16),
        preferred_element_type=jnp.float32,
    )
    rank = jnp.sum(jnp.where(owner_hot, preceding, 0.0), axis=0, keepdims=True).astype(jnp.int32)
    slot = place * cap + rank
    id_values = jnp.broadcast_to((cluster + 1).astype(jnp.float32), (8, rows)).astype(jnp.bfloat16)
    chunk_slot = lax.broadcasted_iota(jnp.int32, (lanes, rows), 0)
    inner_block = lax.broadcasted_iota(jnp.int32, (1, lanes), 1) // cap
    local[1].wait()
    units[...] = normalize(emb_ref[...])
    for chunk in range(send_chunks):
        chosen = (chunk_slot + chunk * lanes == slot).astype(jnp.bfloat16)
        packed = jnp.dot(chosen, units[...], preferred_element_type=jnp.float32)
        send_ref[chunk * lanes : (chunk + 1) * lanes, :] = packed.astype(jnp.bfloat16)
        tile = pair_scores(id_values, chosen)[0:1]
        for within in range(per_chunk):
            own = tile if per_chunk == 1 else jnp.where(inner_block == within, tile, 0.0)
            ids_ref[chunk * per_chunk + within] = own
    local[2].wait()
    new_all[0, 0:new_count, :] = normalize(new_ref[...])

    @pl.when(inner)
    def _():
        pl.semaphore_wait(barrier, greeted + quarter)

    @pl.when(outer)
    def _():
        pl.semaphore_wait(barrier, greeted)

    def new_slots(start, count):
        return new_all.at[0, pl.ds(start * new_count, count * new_count)]

    def layer_new(step):
        return remote(
            new_slots(0, 1),
            new_slots(step, 1),
            new_send.at[step - 1],
            new_recv.at[step - 1],
            far(step * quarter),
        )

    rest_steps = quarter.bit_length() - 1

    def rest_new(index):
        count = 4 << index
        return remote(
            new_slots(0, count),
            new_slots(count, count),
            new_send.at[3 + index],
            new_recv.at[3 + index],
            far(1 << index),
        )

    wide_base = 3 + rest_steps

    def wide_new(index):
        src, dst, step = ((0, 2, 2), (0, 1, 1), (2, 3, 1))[index]
        return remote(
            new_all.at[src],
            new_all.at[dst],
            new_send.at[wide_base + index],
            new_recv.at[wide_base + index],
            near(step),
        )

    cent_copy = remote(
        cent_hbm,
        cent_ref.at[pl.ds(cent_count, cent_count)],
        cent_send.at[0],
        cent_recv.at[0],
        far(quarter),
    )

    def piece_rows(place, index):
        return pl.ds(place * cap + index * piece, piece)

    def landing(place, index):
        block = owner_block(place)
        row = pl.multiple_of(block * cap + index * piece, piece)
        return held.at[pl.ds(row, piece)], data_recv.at[block * pieces + index]

    def direct_copy(place, index):
        target, arrived = landing(place, index)
        return remote(
            send_ref.at[piece_rows(place, index)],
            target,
            data_send.at[place * pieces + index],
            arrived,
            owner_device(place),
        )

    def hop_copy(place, index):
        return remote(
            send_ref.at[piece_rows(place, index)],
            relay_ref.at[piece_rows(place, index)],
            hop_send.at[place * pieces + index],
            hop_recv.at[place * pieces + index],
            related(layer, place % codes),
        )

    def relay_copy(place, index):
        target, arrived = landing(place, index)
        return remote(
            relay_ref.at[piece_rows(place, index)],
            target,
            data_send.at[place * pieces + index],
            arrived,
            related(second_layer if place >= codes else first_layer, 0),
        )

    def id_copy(place):
        block = owner_block(place)
        return remote(
            ids_ref.at[place],
            held_ids.at[block],
            id_send.at[place],
            id_recv.at[block],
            owner_device(place),
        )

    def send_direct(place):
        for index in range(pieces):
            direct_copy(place, index).start()

    def send_hop(place):
        for index in range(pieces):
            hop_copy(place, index).start()

    def relay(place):
        for index in range(pieces):
            hop_copy(place, index).wait_recv()
            relay_copy(place, index).start()

    late_place = self_place + (group_chunks - 1) * per_chunk

    def part_copy(step):
        return remote(
            part.at[step],
            part_in.at[step - 1],
            part_send.at[step - 1],
            part_recv.at[step - 1],
            near(step),
        )

    def best_copy(step):
        return remote(
            best_out,
            best_in.at[step],
            best_send.at[step],
            best_recv.at[step],
            far(step),
        )

    def score_new():
        for step in range(4):
            scores = pair_scores(cent_unit[...], new_all[step])
            top = jnp.max(scores.reshape(scores.shape[0] // 8, 8, group_rows), axis=0)
            top = jnp.max(top, axis=0, keepdims=True)
            for row in range(best_rows):
                part[step, row : row + 1, :] = top[:, row * lanes : (row + 1) * lanes]
        for step in (1, 2, 3):
            part_copy(step).start()

    def spread_best():
        best = part[0]
        for step in (1, 2, 3):
            part_copy(step).wait_recv()
            best = jnp.maximum(best, part_in[step - 1])
        best_out[...] = best
        for step in range(1, clu_count):
            best_copy(step).start()

    def held_copy(block, index):
        return remote(
            send_ref.at[pl.ds(0, piece)],
            held.at[pl.ds(block * cap + index * piece, piece)],
            data_send.at[0],
            data_recv.at[block * pieces + index],
            near(1),
        )

    def held_id_copy(block):
        return remote(
            ids_ref.at[0], held_ids.at[block], id_send.at[0], id_recv.at[block], near(1)
        )

    def forward(spot):
        return (
            remote(
                held_ids.at[pl.ds(spot * per_chunk, per_chunk)],
                held_ids.at[pl.ds((held_chunks + spot) * per_chunk, per_chunk)],
                fwd_id_send.at[spot],
                fwd_id_recv.at[spot],
                near(1),
            ),
            remote(
                held.at[pl.ds(spot * lanes, lanes)],
                held.at[pl.ds(held_rows + spot * lanes, lanes)],
                fwd_send.at[spot],
                fwd_recv.at[spot],
                near(1),
            ),
        )

    def spread_marks(spot):
        row = held_ids[spot * per_chunk]
        for within in range(1, per_chunk):
            row = row + held_ids[spot * per_chunk + within]
        marks[pl.ds(spot * lanes, lanes), :] = jnp.transpose(
            jnp.broadcast_to(row, (lanes, lanes))
        )
        if spot < held_chunks:
            stage, part_of = divmod(spot, 2)
            id_rows[stage, :, pl.ds(part_of * lanes, lanes)] = jnp.broadcast_to(row, (8, lanes))

    def pass_on(spot):
        for within in range(per_chunk):
            block = spot * per_chunk + within
            if block > 0:
                held_id_copy(block).wait_recv()
                for index in range(pieces):
                    held_copy(block, index).wait_recv()
        for copy in forward(spot):
            copy.start()
        spread_marks(spot)

    def receive(spot):
        for copy in forward(spot):
            copy.wait_recv()
        spread_marks(held_chunks + spot)

    def tile_pair(start, count, right, diagonal=False):
        if not isinstance(start, int):
            start = pl.multiple_of(start, count)
        left_rows = pl.ds(start, count)
        right_start = right * stage_rows
        if not isinstance(right_start, int):
            right_start = pl.multiple_of(right_start, stage_rows)
        mark = marks[left_rows, :]
        matched = jnp.concatenate([mark, mark], axis=1) == id_rows[right][0:1]
        if diagonal:
            row_id = lax.broadcasted_iota(jnp.int32, (stage_rows, stage_rows), 0)
            col_id = lax.broadcasted_iota(jnp.int32, (stage_rows, stage_rows), 1)
            matched = matched & (row_id != col_id)
        scores = pair_scores(held[left_rows, :], held[pl.ds(right_start, stage_rows), :])
        kept = jnp.where(matched, scores, -1.0)
        top = jnp.max(kept.reshape(count // 8, 8, stage_rows), axis=0)
        acc[right] = jnp.maximum(acc[right], top)

    def stage_diagonal(stage):
        tile_pair(stage * stage_rows, stage_rows, stage, diagonal=True)
        tile_pair(held_rows + stage * stage_rows, stage_rows, stage)

    def compute(stage):
        stage_diagonal(stage)

        def body(other, carry):
            tile_pair(stage * stage_rows, stage_rows, other)
            tile_pair(held_rows + stage * stage_rows, stage_rows, other)
            tile_pair(other * stage_rows, stage_rows, stage)
            tile_pair(held_rows + other * stage_rows, stage_rows, stage)
            return carry

        if stage:
            lax.fori_loop(0, stage, body, 0)

    def take(stage):
        pass_on(2 * stage)
        pass_on(2 * stage + 1)
        receive(2 * stage)
        receive(2 * stage + 1)

    last = stage_count - 1

    def chunk_rows(spot):
        def body(other, carry):
            tile_pair(spot * lanes, lanes, other)
            tile_pair(held_rows + spot * lanes, lanes, other)
            return carry

        lax.fori_loop(0, last, body, 0)

    def last_columns():
        def body(other, carry):
            tile_pair(other * stage_rows, stage_rows, last)
            tile_pair(held_rows + other * stage_rows, stage_rows, last)
            return carry

        lax.fori_loop(0, last, body, 0)

    def message_copy(block):
        spot, within = divmod(block, per_chunk)
        to_layer, chunk = held_source(spot)
        place = chunk * per_chunk + within
        return remote(
            message.at[spot],
            message_in.at[place],
            msg_send.at[block],
            msg_recv.at[place],
            related(to_layer, place % codes),
        )

    def message_copy_in(place):
        return remote(
            message.at[0], message_in.at[place], msg_send.at[0], msg_recv.at[place], near(1)
        )

    @pl.when(inner)
    def _():
        for step in (1, 2):
            layer_new(step).start()
        for place in range(clu_count):
            if place != self_place:
                id_copy(place).start()
        for code in range(codes):
            send_direct(code)
            if code and self_place + code < late_place:
                send_direct(self_place + code)
        cent_copy.start()
        held[0:cap, :] = send_ref[self_place * cap : (self_place + 1) * cap, :]
        held_ids[0] = ids_ref[self_place]
        acc[...] = jnp.full(acc.shape, -1.0, jnp.float32)
        for stage in range(last):
            pass_on(2 * stage)
            if 2 * stage == spots_middle[-1]:
                for place in range(late_place, clu_count):
                    send_direct(place)
            pass_on(2 * stage + 1)
            receive(2 * stage)
            receive(2 * stage + 1)
            compute(stage)
        pass_on(2 * last)
        receive(2 * last)
        chunk_rows(2 * last)
        pass_on(2 * last + 1)
        receive(2 * last + 1)
        chunk_rows(2 * last + 1)
        stage_diagonal(last)
        last_columns()
        for stage in range(stage_count):
            final = jnp.max(acc[stage], axis=0, keepdims=True)
            for part_of in range(2):
                message[2 * stage + part_of] = final[:, part_of * lanes : (part_of + 1) * lanes]
        for block in range(1, 2 * clu_count):
            message_copy(block).start()
        message_in[self_place] = message[0]
        for spot in range(held_chunks):
            for copy in forward(spot):
                copy.wait_send()
        cent_copy.wait_send()
        for step in (1, 2):
            layer_new(step).wait_send()
        for place in range(clu_count):
            if place != self_place:
                id_copy(place).wait_send()
                for index in range(pieces):
                    direct_copy(place, index).wait_send()
        for step in range(1, clu_count):
            if step // quarter in (1, 2):
                best_copy(step).wait_recv()
        for block in range(1, 2 * clu_count):
            message_copy(block).wait_send()

    @pl.when(outer)
    def _():
        layer_new(3).start()
        for place in range(clu_count):
            id_copy(place).start()
        send_direct(0)
        for code in range(1, codes):
            send_hop(code)
        local_cent.wait()
        cent_unit[0:cent_count, :] = normalize(cent_ref[0:cent_count, :])
        for code in range(1, codes // 2 + 1):
            relay(code)
        for step in (1, 2, 3):
            layer_new(step).wait_recv()
        if rest_steps:
            rest_new(0).start()
        for code in range(codes // 2 + 1, codes):
            relay(code)
        send_direct(codes)
        for code in range(1, codes):
            send_hop(codes + code)
        for index in range(rest_steps):
            rest_new(index).wait_recv()
            if index + 1 < rest_steps:
                rest_new(index + 1).start()
        wide_new(0).start()
        for code in range(1, codes):
            relay(codes + code)
        cent_copy.wait_recv()
        cent_unit[cent_count:, :] = normalize(cent_ref[cent_count:, :])
        wide_new(0).wait_recv()
        wide_new(1).start()
        wide_new(2).start()
        wide_new(1).wait_recv()
        wide_new(2).wait_recv()
        score_new()
        spread_best()
        layer_new(3).wait_send()
        for index in range(rest_steps):
            rest_new(index).wait_send()
        for index in range(3):
            wide_new(index).wait_send()
        for step in (1, 2, 3):
            part_copy(step).wait_send()
        for step in range(1, clu_count):
            best_copy(step).wait_send()
            if step // quarter == 3 or step // quarter == 0:
                best_copy(step).wait_recv()
        for place in range(clu_count):
            id_copy(place).wait_send()
            for index in range(pieces):
                if place % codes:
                    hop_copy(place, index).wait_send()
                    relay_copy(place, index).wait_send()
                else:
                    direct_copy(place, index).wait_send()
        message_copy_in(self_place).wait_recv()

    def best_piece(source, step):
        layer_step, rest_step = divmod(step, quarter)
        start = (rest_step * 4 + layer_step) * new_count
        row = start // lanes
        return source[row : row + 1, start % lanes : start % lanes + new_count]

    @pl.when(inner)
    def _():
        best = None
        for step in range(quarter, 3 * quarter):
            found = best_piece(best_in[step], step)
            best = found if best is None else jnp.maximum(best, found)
        best_ref[...] = best

    @pl.when(outer)
    def _():
        best = best_piece(best_out[...], 0)
        for step in (*range(1, quarter), *range(3 * quarter, clu_count)):
            best = jnp.maximum(best, best_piece(best_in[step], step))
        best_ref[...] = best

    for place in range(clu_count):
        if place != self_place:
            message_copy_in(place).wait_recv()

    row_list = []
    for chunk in range(send_chunks):
        row = message_in[chunk * per_chunk]
        for within in range(1, per_chunk):
            row = jnp.where(inner_block == within, message_in[chunk * per_chunk + within], row)
        row_list.append(row)
    columns = jnp.transpose(
        jnp.concatenate([jnp.broadcast_to(row, (16, lanes)) for row in row_list], axis=0)
    )
    total = jnp.zeros(slot.shape, jnp.float32)
    for chunk in range(send_chunks):
        column = columns[:, chunk * 16 : chunk * 16 + 1]
        total = total + jnp.sum(
            jnp.where(chunk_slot + chunk * lanes == slot, column, 0.0), axis=0, keepdims=True
        )
    dup_ref[...] = total


def shards(embeddings, cluster_of, new_rows, centroids):
    clu_count = lax.axis_size("clu")
    rows, width = embeddings.shape
    new_count = new_rows.shape[0]
    cap = 2 * rows // clu_count
    slots = clu_count * cap
    assert slots == send_chunks * lanes
    assert lax.axis_size("grp") == 4
    vmem = pl.BlockSpec(memory_space=pltpu.VMEM)
    anywhere = pl.BlockSpec(memory_space=pl.ANY)
    dma = pltpu.SemaphoreType.DMA
    group_rows = clu_count * new_count
    best_rows = group_rows // lanes
    cent_count = centroids.shape[0]
    new_steps = 3 + (clu_count // 4).bit_length() - 1 + 3
    dup, best = pl.pallas_call(
        functools.partial(exchange_kernel, clu_count, cap, new_count),
        out_shape=(
            jax.ShapeDtypeStruct((1, rows), jnp.float32),
            jax.ShapeDtypeStruct((1, new_count), jnp.float32),
        ),
        in_specs=[anywhere] * 4,
        out_specs=(vmem, vmem),
        scratch_shapes=[
            pltpu.VMEM((rows, width), jnp.bfloat16),
            pltpu.VMEM((1, rows), jnp.int32),
            pltpu.VMEM((new_count, width), jnp.bfloat16),
            pltpu.VMEM((2 * cent_count, width), jnp.bfloat16),
            pltpu.VMEM((rows, width), jnp.bfloat16),
            pltpu.VMEM((slots, width), jnp.bfloat16),
            pltpu.VMEM((slots, width), jnp.bfloat16),
            pltpu.VMEM((clu_count, 1, lanes), jnp.float32),
            pltpu.VMEM((2 * held_rows, width), jnp.bfloat16),
            pltpu.VMEM((4 * clu_count, 1, lanes), jnp.float32),
            pltpu.VMEM((2 * held_rows, lanes), jnp.float32),
            pltpu.VMEM((stage_count, 8, stage_rows), jnp.float32),
            pltpu.VMEM((stage_count, 8, stage_rows), jnp.float32),
            pltpu.VMEM((4, group_rows, width), jnp.bfloat16),
            pltpu.VMEM((2 * cent_count, width), jnp.bfloat16),
            pltpu.VMEM((4, best_rows, lanes), jnp.float32),
            pltpu.VMEM((3, best_rows, lanes), jnp.float32),
            pltpu.VMEM((best_rows, lanes), jnp.float32),
            pltpu.VMEM((clu_count, best_rows, lanes), jnp.float32),
            pltpu.VMEM((held_chunks, 1, lanes), jnp.float32),
            pltpu.VMEM((clu_count, 1, lanes), jnp.float32),
            dma((4,)),
            dma((2 * clu_count,)),
            dma((4 * clu_count,)),
            dma((2 * clu_count,)),
            dma((2 * clu_count,)),
            dma((clu_count,)),
            dma((2 * clu_count,)),
            dma((held_chunks,)),
            dma((held_chunks,)),
            dma((held_chunks,)),
            dma((held_chunks,)),
            dma((new_steps,)),
            dma((new_steps,)),
            dma((3,)),
            dma((3,)),
            dma((clu_count,)),
            dma((clu_count,)),
            dma((2 * clu_count,)),
            dma((clu_count,)),
            dma((1,)),
            dma((1,)),
        ],
        compiler_params=pltpu.CompilerParams(
            collective_id=0, has_side_effects=True, vmem_limit_bytes=67043328
        ),
        name="exchange",
    )(embeddings, cluster_of.reshape(1, rows), new_rows, centroids)
    return (dup.reshape(rows), best.reshape(new_count))


def solution(mesh):
    return jax.shard_map(
        shards,
        mesh=mesh,
        in_specs=(
            P(("clu", "grp"), None),
            P(("clu", "grp")),
            P(("clu", "grp"), None),
            P(("clu", "grp"), None),
        ),
        out_specs=(P(("clu", "grp")), P(("clu", "grp"))),
        check_vma=False,
    )
```

time: 64.5 us -> 75.4 us (1.17)
  Pallas kernels: 61.9 us -> 72.8 us
    pallas_call x1, Pallas kernels: 61.9 us -> 72.8 us  [shards(): pl.pallas_call(functools.partial(exchange_kernel, clu_count, cap, new_cou...]
where the time goes in v1:
time: 75.4 us; the launch traced here: 75.3 us
  Pallas kernels  72.8 us (97%)
  local copies, waits for them, and re-layouts  1.8 us (2%)
    pallas_call x1, Pallas kernels, shards(): pl.pallas_call(functools.partial(exchange_kernel, clu_count, cap, new_cou...  72.8 us
    unnamed x6, local copies, waits for them, and re-layouts  1.8 us

profile of v1, /device:TPU:0, one launch (start us, length us, event | category | flops | bytes accessed | tf_op | source)
XLA Modules:
  0.0 75.3 jit_solution(6994182041793940260)
XLA Ops:
  0.6 72.8 %exchange.1 = (f32[1,512]{1,0:T(1,128)}, f32[1,16]{1,0:T(1,128)}) custom-call(bf16[512,768]{1,0:T(8,128)(2,1)} %emb_hbm.1, s32[1,512]{1,0:T(1,128)} %bitcast.3, bf16[16,768]{1,0:T(8,128)(2,1)} %new_hbm.1, bf16[256,768]{1,0:T(8,128)(2,1)} %cent_hbm.1), custom_call_target="tpu_custom_call" | custom-call | tf_op jit(solution)/shard_map/exchange/pallas_call | solution.py:681
  73.4 0.0 copy-start
  73.5 0.7 copy-done
  74.1 0.0 copy-start.1
  74.1 0.6 copy.8
  74.7 0.1 copy-done.1
  74.8 0.5 copy.9
Async XLA Ops:
  73.4 0.7 copy-start
  74.1 0.6 copy-start.1

commit v2 on v0

--- a/solution.py
+++ b/solution.py
@@ -179,19 +179,15 @@
     slot = place * cap + rank
     id_values = jnp.broadcast_to((cluster + 1).astype(jnp.float32), (8, rows)).astype(jnp.bfloat16)
     chunk_slot = lax.broadcasted_iota(jnp.int32, (lanes, rows), 0)
-    inner_block = lax.broadcasted_iota(jnp.int32, (8, lanes), 1) // cap
+    inner_block = lax.broadcasted_iota(jnp.int32, (1, lanes), 1) // cap
     local[2].wait()
     units[...] = normalize(emb_ref[...])
-    pl.semaphore_wait(barrier, clu_count - 1 + 3)
-    for copy in new_copies:
-        copy.start()
-
     def pack(chunk):
         chosen = (chunk_slot + chunk * lanes == slot).astype(jnp.bfloat16)
         packed = jnp.dot(chosen, units[...], preferred_element_type=jnp.float32).astype(
             jnp.bfloat16
         )
-        tile = pair_scores(id_values, chosen)
+        tile = pair_scores(id_values, chosen)[0:1]
         for inner in range(per_chunk):
             block = chunk * per_chunk + inner
             if per_chunk == 1:
@@ -217,11 +213,13 @@
         tile = held_ids[kind, chunk * per_chunk]
         for inner in range(1, per_chunk):
             tile = tile + held_ids[kind, chunk * per_chunk + inner]
-        square = jnp.concatenate([tile] * (lanes // 8), axis=0)
+        square = jnp.broadcast_to(tile, (lanes, lanes))
         marks[pl.ds(chunk_row(chunk, kind), half), :] = jnp.transpose(square)
         if kind < 2:
             stage, part_of = divmod(chunk, 2)
-            id_rows[stage, kind, :, pl.ds(part_of * half, half)] = tile
+            id_rows[stage, kind, :, pl.ds(part_of * half, half)] = jnp.broadcast_to(
+                tile, (8, half)
+            )
 
     def pass_on(chunk):
         for inner in range(per_chunk):
@@ -252,8 +250,8 @@
             forwards[chunk, kind] = (ids, data)
         spread_marks(chunk, 0)
 
-    def receive(chunk):
-        for kind in (1, 2):
+    def receive(chunk, kinds=(1, 2)):
+        for kind in kinds:
             ids, data = forwards[chunk, kind]
             ids.wait_recv()
             data.wait_recv()
@@ -313,8 +311,11 @@
                 own_pair(kind, step, last)
             return carry
 
-        def other_rows(step, carry):
+        def mate_rows(step, carry):
             own_pair(1, last, step)
+            return carry
+
+        def cross_rows(step, carry):
             own_pair(2, last, step)
             mate_pair(last, step)
             return carry
@@ -325,12 +326,16 @@
 
         lax.fori_loop(0, stage_count, own_rows, 0)
         lax.fori_loop(0, last, own_cols, 0)
-        receive(2 * last)
-        receive(2 * last + 1)
+        receive(2 * last, (1,))
+        receive(2 * last + 1, (1,))
         lax.fori_loop(0, last, mate_cols, 0)
-        lax.fori_loop(0, stage_count, other_rows, 0)
+        lax.fori_loop(0, stage_count, mate_rows, 0)
+        receive(2 * last, (2,))
+        receive(2 * last + 1, (2,))
+        lax.fori_loop(0, stage_count, cross_rows, 0)
 
     group_rows = clu_count * new_count
+    best_rows = group_rows // lanes
     cross_new = remote(
         new_held.at[0], new_held.at[2], wide_send.at[0], wide_recv.at[0], near(2)
     )
@@ -374,17 +379,15 @@
         for copy in part_copies:
             copy.start()
 
-    pack(0)
-    for chunk in range(1, chunk_count):
+    for chunk in range(chunk_count):
         pack(chunk)
-        if chunk == 1:
-            if per_chunk > 1:
-                dispatch(0)
-        else:
-            dispatch(chunk - 1)
+    pl.semaphore_wait(barrier, clu_count - 1 + 3)
+    for copy in new_copies:
+        copy.start()
+    for chunk in range(chunk_count):
+        dispatch(chunk)
     own_acc[...] = jnp.full(own_acc.shape, -1.0, jnp.float32)
     mate_acc[...] = jnp.full(mate_acc.shape, -1.0, jnp.float32)
-    dispatch(chunk_count - 1)
     pass_on(0)
     local[3].wait()
     cent_unit[...] = normalize(cent_ref[...])
@@ -415,10 +418,8 @@
             jnp.maximum(own_acc[stage], mate_in[stage]), axis=0, keepdims=True
         )
         for part_of in range(2):
-            message[2 * stage + part_of, 0:8, :] = jnp.broadcast_to(
-                final[:, part_of * half : (part_of + 1) * half], (8, lanes)
-            )
-            message[2 * stage + part_of, 8:, :] = cent_best
+            message[2 * stage + part_of, 0:1, :] = final[:, part_of * half : (part_of + 1) * half]
+            message[2 * stage + part_of, 1:, :] = cent_best[0:best_rows]
     messages = []
     for block in range(1, clu_count):
         copy = remote(
@@ -464,7 +465,7 @@
     best = None
     for block in range(clu_count):
         start = block * new_count
-        row = 8 + start // lanes
+        row = 1 + start // lanes
         piece = message_in[block, row : row + 1, :][:, start % lanes : start % lanes + new_count]
         best = piece if best is None else jnp.maximum(best, piece)
     best_ref[...] = best
@@ -498,9 +499,9 @@
             pltpu.VMEM(centroids.shape, jnp.bfloat16),
             pltpu.VMEM((rows, width), jnp.bfloat16),
             pltpu.VMEM((slots, width), jnp.bfloat16),
-            pltpu.VMEM((clu_count, 8, lanes), jnp.float32),
+            pltpu.VMEM((clu_count, 1, lanes), jnp.float32),
             pltpu.VMEM((3 * slots, width), jnp.bfloat16),
-            pltpu.VMEM((3, clu_count, 8, lanes), jnp.float32),
+            pltpu.VMEM((3, clu_count, 1, lanes), jnp.float32),
             pltpu.VMEM((3 * slots, lanes), jnp.float32),
             pltpu.VMEM((stage_count, 2, 8, stage_rows), jnp.float32),
             pltpu.VMEM((stage_count, 8, stage_rows), jnp.float32),
@@ -510,8 +511,8 @@
             pltpu.VMEM(centroids.shape, jnp.bfloat16),
             pltpu.VMEM((4, 8, lanes), jnp.float32),
             pltpu.VMEM((3, 8, lanes), jnp.float32),
-            pltpu.VMEM((chunk_count, 16, lanes), jnp.float32),
-            pltpu.VMEM((clu_count, 16, lanes), jnp.float32),
+            pltpu.VMEM((chunk_count, 1 + group_rows // lanes, lanes), jnp.float32),
+            pltpu.VMEM((clu_count, 1 + group_rows // lanes, lanes), jnp.float32),
             dma((4,)),
             dma((clu_count,)),
             dma((clu_count,)),

time: 64.5 us -> 63.1 us (0.978)
  Pallas kernels: 61.9 us -> 60.5 us
    pallas_call x1, Pallas kernels: 61.9 us -> 60.5 us  [shards(): pl.pallas_call(functools.partial(exchange_kernel, clu_count, cap, new_cou...]
where the time goes in v2:
time: 63.1 us; the launch traced here: 62.9 us
  Pallas kernels  60.5 us (96%)
  local copies, waits for them, and re-layouts  1.8 us (3%)
  between operations  0.65 us (1%)
    pallas_call x1, Pallas kernels, shards(): pl.pallas_call(functools.partial(exchange_kernel, clu_count, cap, new_cou...  60.5 us
    unnamed x6, local copies, waits for them, and re-layouts  1.8 us

profile of v2, /device:TPU:0, one launch (start us, length us, event | category | flops | bytes accessed | tf_op | source)
XLA Modules:
  0.0 62.9 jit_solution(1754292676249684833)
XLA Ops:
  0.6 60.5 %exchange.1 = (f32[1,512]{1,0:T(1,128)}, f32[1,16]{1,0:T(1,128)}) custom-call(bf16[512,768]{1,0:T(8,128)(2,1)} %emb_hbm.1, s32[1,512]{1,0:T(1,128)} %bitcast.3, bf16[16,768]{1,0:T(8,128)(2,1)} %new_hbm.1, bf16[256,768]{1,0:T(8,128)(2,1)} %cent_hbm.1), custom_call_target="tpu_custom_call" | custom-call | tf_op jit(solution)/shard_map/exchange/pallas_call | solution.py:487
  61.1 0.0 copy-start
  61.1 0.7 %copy-done = f32[1,512]{1,0:T(1,128)S(1)} copy-done((f32[1,512]{1,0:T(1,128)S(1)}, f32[1,512]{1,0:T(1,128)}, u32[]{:S(2)}) %copy-start) | copy-done | bytes 2072
  61.8 0.0 copy-start.1
  61.8 0.6 copy.8
  62.4 0.1 copy-done.1
  62.4 0.5 copy.9
Async XLA Ops:
  61.1 0.7 %copy-start = (f32[1,512]{1,0:T(1,128)S(1)}, f32[1,512]{1,0:T(1,128)}, u32[]{:S(2)}) copy-start(f32[1,512]{1,0:T(1,128)} %get-tuple-element.4) | copy-start | bytes 6148
  61.8 0.6 %copy-start.1 = (f32[1,16]{1,0:T(1,128)S(1)}, f32[1,16]{1,0:T(1,128)}, u32[]{:S(2)}) copy-start(f32[1,16]{1,0:T(1,128)} %get-tuple-element.5) | copy-start | bytes 196

commit v3 on v2

--- a/solution.py
+++ b/solution.py
@@ -384,7 +384,7 @@
     pl.semaphore_wait(barrier, clu_count - 1 + 3)
     for copy in new_copies:
         copy.start()
-    for chunk in range(chunk_count):
+    for chunk in (0, 1, 2, 3, 4):
         dispatch(chunk)
     own_acc[...] = jnp.full(own_acc.shape, -1.0, jnp.float32)
     mate_acc[...] = jnp.full(mate_acc.shape, -1.0, jnp.float32)
@@ -392,12 +392,15 @@
     local[3].wait()
     cent_unit[...] = normalize(cent_ref[...])
     pass_on(1)
+    dispatch(5)
     new_first()
     pass_on(2)
     pass_on(3)
+    dispatch(6)
     new_second()
     compute(0)
     pass_on(4)
+    dispatch(7)
     new_third()
     pass_on(5)
     compute(1)

time: 63.1 us -> 62.3 us (0.987)
  Pallas kernels: 60.5 us -> 59.7 us
    pallas_call x1, Pallas kernels: 60.5 us -> 59.7 us  [shards(): pl.pallas_call(functools.partial(exchange_kernel, clu_count, cap, new_cou...]
where the time goes in v3:
time: 62.3 us; the launch traced here: 62.2 us
  Pallas kernels  59.7 us (96%)
  local copies, waits for them, and re-layouts  1.8 us (3%)
  between operations  0.65 us (1%)
    pallas_call x1, Pallas kernels, shards(): pl.pallas_call(functools.partial(exchange_kernel, clu_count, cap, new_cou...  59.7 us
    unnamed x6, local copies, waits for them, and re-layouts  1.8 us

profile of v3, /device:TPU:0, one launch (start us, length us, event | category | flops | bytes accessed | tf_op | source)
XLA Modules:
  0.0 62.2 jit_solution(760477919999362989)
XLA Ops:
  0.6 59.7 %exchange.1 = (f32[1,512]{1,0:T(1,128)}, f32[1,16]{1,0:T(1,128)}) custom-call(bf16[512,768]{1,0:T(8,128)(2,1)} %emb_hbm.1, s32[1,512]{1,0:T(1,128)} %bitcast.3, bf16[16,768]{1,0:T(8,128)(2,1)} %new_hbm.1, bf16[256,768]{1,0:T(8,128)(2,1)} %cent_hbm.1), custom_call_target="tpu_custom_call" | custom-call | tf_op jit(solution)/shard_map/exchange/pallas_call | solution.py:490
  60.3 0.0 copy-start
  60.4 0.7 %copy-done = f32[1,512]{1,0:T(1,128)S(1)} copy-done((f32[1,512]{1,0:T(1,128)S(1)}, f32[1,512]{1,0:T(1,128)}, u32[]{:S(2)}) %copy-start) | copy-done | bytes 2072
  61.0 0.0 copy-start.1
  61.0 0.6 copy.8
  61.6 0.1 copy-done.1
  61.7 0.5 copy.9
Async XLA Ops:
  60.3 0.7 %copy-start = (f32[1,512]{1,0:T(1,128)S(1)}, f32[1,512]{1,0:T(1,128)}, u32[]{:S(2)}) copy-start(f32[1,512]{1,0:T(1,128)} %get-tuple-element.4) | copy-start | bytes 6148
  61.0 0.6 %copy-start.1 = (f32[1,16]{1,0:T(1,128)S(1)}, f32[1,16]{1,0:T(1,128)}, u32[]{:S(2)}) copy-start(f32[1,16]{1,0:T(1,128)} %get-tuple-element.5) | copy-start | bytes 196
